TPU v7x, 256 devices: a whole 4x4x8 slice. The times are simulated.
256 devices in a mesh: sub: 64 (over z, y, core), grp: 4 (over x).
Axes of the slice: x: 4, y: 4, z: 8, core: 2. Of those that a mesh axis runs over, the one named last changes fastest.
Arguments:
- coarse: float32 [6144, 128], P(('sub', 'grp')), may hold values from -6 to 6
- corner_idx: int32 [256, 24], P(('sub', 'grp')), may hold values from 0 to 6143, as said below
- coupling: bfloat16 [393216, 24], P(('sub', 'grp')), may hold values from -1.25 to 1.25
- force: bfloat16 [131072, 3, 128], P(('sub', 'grp')), may hold values from -6 to 6
- panel_inv: bfloat16 [1024, 384, 384], P(('sub', 'grp')), as said below
- panel_nodes: int32 [256, 4], P(('sub', 'grp')), may hold values from 64 to 128, as said below
- strain_disp: bfloat16 [6, 24, 32768], P(None, None, ('sub', 'grp')), may hold values from -1.25 to 1.25
- modulus: float32 [32768], P(('sub', 'grp')), may hold values from 0.5 to 4
- connect: int32 [8, 32768], P(None, ('sub', 'grp')), may hold values from 0 to 511, as said below
- interface: int32 [256, 224], P(('sub', 'grp')), may hold values from 0 to 511, as said below
- nodal_volume: float32 [131072], P(('sub', 'grp')), may hold values from 4 to 16
Outputs:
- displacement: bfloat16 [131072, 3, 128], P(('sub', 'grp'))
- nodal_stress: bfloat16 [131072, 6, 128], P(('sub', 'grp'))
Inputs may be any that keep to these rules, and one draw needn't show every extreme that they name: `corner_idx`: the rows of subdomain (s, g) lie in the coarse blocks of subdomains (s', g') with |s' - s| <= 1 that exist, including blocks of all grp indices; they come in triples of consecutive rows. `panel_nodes`: every subdomain has one panel with exactly 128 live nodes and one with 64. `connect`: every entry is a live node of its subdomain (slot j < panel_nodes of its panel). `interface`: each row holds 224 distinct live nodes as eight lists: sub-lo (64), sub-hi (64), grp-lo (32), grp-hi (32), then edges ll, lh, hl, hh (8 each; first letter the sub side, second the grp side). Entry k of a list of (s, g) is the same physical node as entry k of the facing list of each neighbour: sub-hi with sub-lo of (s + 1, g), grp-hi with grp-lo of (s, g + 1); edge (x, y) with the edge of the neighbour across it that has the opposite letter on each side crossed. `panel_inv`: given inverses of the padded panels.
All inputs are finite; a program needn't handle non-finite values.
Results may differ from a plain program's by a relative error of at most 0.0058.
Values sent between devices are 32-bit elements; how exact they have to be, the bound alone decides.
A program may use at most 64 MiB of HBM per device.

v0:
```python
import jax
import jax.numpy as jnp
from jax import lax
from jax.sharding import PartitionSpec as P

NIS = 64
NIG = 32
NED = 8
POISSON = 0.3


def padded(block, sides, width):
    for axis, dim in sides:
        count = lax.axis_size(axis)
        forward = [(i, i + 1) for i in range(count - 1)]
        backward = [(target, source) for source, target in forward]
        low = lax.ppermute(
            lax.slice_in_dim(block, block.shape[dim] - width, None, axis=dim), axis, forward
        )
        high = lax.ppermute(lax.slice_in_dim(block, 0, width, axis=dim), axis, backward)
        block = jnp.concatenate([low, block, high], axis=dim)
    return block


def iso_matrix():
    lame_first = POISSON / ((1.0 + POISSON) * (1.0 - 2.0 * POISSON))
    shear_mod = 0.5 / (1.0 + POISSON)
    upper_block = jnp.full((3, 3), lame_first, jnp.float32) + jnp.eye(3, dtype=jnp.float32) * (
        2.0 * shear_mod
    )
    shear_block = jnp.eye(3, dtype=jnp.float32) * shear_mod
    zero_block = jnp.zeros((3, 3), jnp.float32)
    return jnp.concatenate(
        [
            jnp.concatenate([upper_block, zero_block], 1),
            jnp.concatenate([zero_block, shear_block], 1),
        ],
        0,
    )


def shards(
    coarse,
    corner_idx,
    coupling,
    force,
    panel_inv,
    panel_nodes,
    strain_disp,
    modulus,
    connect,
    interface,
    nodal_volume,
):
    group_rows = lax.all_gather(coarse, "grp", axis=0, tiled=True)
    block_rows = group_rows.shape[0]
    nearby = padded(group_rows, (("sub", 0),), block_rows)
    offset = (lax.axis_index("sub") - 1) * block_rows
    local_rows = corner_idx[0] - offset
    selector = (local_rows[:, None] == jnp.arange(3 * block_rows, dtype=jnp.int32)[None, :]).astype(
        jnp.float32
    )
    corner_vals = jnp.dot(selector, nearby, precision=lax.Precision.HIGHEST)
    node_count = force.shape[0]
    load_cases = force.shape[2]
    panels = panel_inv.shape[0]
    panel_rows = panel_inv.shape[1]
    correction = jnp.dot(coupling.astype(jnp.float32), corner_vals, precision=lax.Precision.HIGHEST)
    live_mask = jnp.arange(panel_rows)[None, :] < 3 * panel_nodes[0][:, None]
    reduced = (force.reshape(3 * node_count, load_cases).astype(jnp.float32) - correction).reshape(
        panels, panel_rows, load_cases
    )
    reduced = jnp.where(live_mask[:, :, None], reduced, 0.0).astype(jnp.bfloat16)
    solved = jnp.einsum("prc,pcl->prl", panel_inv, reduced, preferred_element_type=jnp.float32)
    displaced = (
        jnp.where(live_mask[:, :, None], solved, 0.0)
        .astype(jnp.bfloat16)
        .reshape(node_count, 3 * load_cases)
    )
    elem_count = connect.shape[1]
    element = displaced[connect.T].reshape(elem_count, 24, load_cases)
    strain = jnp.einsum("ije,ejl->eil", strain_disp, element, preferred_element_type=jnp.float32)
    stress = (
        jnp.einsum("ik,ekl->eil", iso_matrix(), strain, precision=lax.Precision.HIGHEST)
        * modulus[:, None, None]
    )
    node_range = jnp.arange(node_count, dtype=jnp.int32)
    incidence = jnp.sum(
        (connect[:, None, :] == node_range[None, :, None]).astype(jnp.float32), axis=0
    )
    partial_value = jnp.dot(
        incidence, stress.reshape(elem_count, 6 * load_cases), precision=lax.Precision.HIGHEST
    ).reshape(node_count, 6, load_cases)
    node_ids = interface[0]
    picker = (node_ids[:, None] == node_range[None, :]).astype(jnp.float32)
    iface_rows = jnp.dot(
        picker, partial_value.reshape(node_count, 6 * load_cases), precision=lax.Precision.HIGHEST
    ).reshape(-1, 6, load_cases)
    start_edge = 2 * NIS + 2 * NIG
    faces_sub = iface_rows[: 2 * NIS].reshape(2, NIS, 6, load_cases)
    near_sub = padded(faces_sub, (("sub", 0),), 1)
    faces_sub = faces_sub + jnp.stack([near_sub[0], near_sub[3]])
    faces_grp = iface_rows[2 * NIS : start_edge].reshape(2, NIG, 6, load_cases)
    near_grp = padded(faces_grp, (("grp", 0),), 1)
    faces_grp = faces_grp + jnp.stack([near_grp[0], near_grp[3]])
    edge_block = iface_rows[start_edge:].reshape(2, 2, NED, 6, load_cases)
    beside_all = padded(edge_block, (("sub", 0), ("grp", 1)), 1)
    along_sub = jnp.stack([beside_all[0, 1:3], beside_all[3, 1:3]])
    along_grp = jnp.stack([beside_all[1:3, 0], beside_all[1:3, 3]], axis=1)
    diagonal = jnp.stack(
        [
            jnp.stack([beside_all[0, 0], beside_all[0, 3]]),
            jnp.stack([beside_all[3, 0], beside_all[3, 3]]),
        ]
    )
    edge_block = edge_block + along_sub + along_grp + diagonal
    summed_rows = jnp.concatenate(
        [
            faces_sub.reshape(-1, 6, load_cases),
            faces_grp.reshape(-1, 6, load_cases),
            edge_block.reshape(-1, 6, load_cases),
        ]
    )
    placed = jnp.dot(
        picker.T, summed_rows.reshape(-1, 6 * load_cases), precision=lax.Precision.HIGHEST
    ).reshape(node_count, 6, load_cases)
    on_face = jnp.sum(picker, axis=0) > 0.5
    summed = jnp.where(on_face[:, None, None], placed, partial_value)
    stress_out = (summed / nodal_volume[:, None, None]).astype(jnp.bfloat16)
    return (displaced.reshape(node_count, 3, load_cases), stress_out)


def solution(mesh):
    placed = (
        P(("sub", "grp"), None),
        P(("sub", "grp"), None),
        P(("sub", "grp"), None),
        P(("sub", "grp"), None, None),
        P(("sub", "grp"), None, None),
        P(("sub", "grp"), None),
        P(None, None, ("sub", "grp")),
        P(("sub", "grp")),
        P(None, ("sub", "grp")),
        P(("sub", "grp"), None),
        P(("sub", "grp")),
    )
    return jax.shard_map(
        shards,
        mesh=mesh,
        in_specs=placed,
        out_specs=(P(("sub", "grp"), None, None), P(("sub", "grp"), None, None)),
        check_vma=False,
    )
```

profile of v0, /device:TPU:123, one launch (start us, length us, event | category | flops | bytes accessed | tf_op | source)
XLA Modules:
  0.0 98.0 jit_solution(14922059316060356889)
XLA Ops:
  0.6 9.4 %all_gather.3 = f32[96,128]{1,0:T(8,128)S(1)} all-gather(f32[24,128]{1,0:T(8,128)} %param.11), channel_id=1, replica_groups=mesh['sub'=64,'grp'=4] {'grp'}, dimensions={0}, use_global_device_ids=true | all-gather | bytes 61440 | tf_op jit(solution)/shard_map/all_gather | solution.py:55
  10.1 5.5 %collective-permute-start.1 = (f32[96,128]{1,0:T(8,128)S(1)}, f32[96,128]{1,0:T(8,128)S(1)}, u32[]{:S(2)}, u32[]{:S(2)}) collective-permute-start(f32[96,128]{1,0:T(8,128)S(1)} %all_gather.3), channel_id=1, source_target_pairs={{4,0},{8,4},{12,8},{16,12},{20,16},{24,20},{28,24},{32,28},{36,32}... | collective-permute-start | bytes 147464 | tf_op jit(solution)/shard_map/ppermute | solution.py:20
  15.5 4.3 %collective-permute-start = (f32[96,128]{1,0:T(8,128)S(1)}, f32[96,128]{1,0:T(8,128)S(1)}, u32[]{:S(2)}, u32[]{:S(2)}) collective-permute-start(f32[96,128]{1,0:T(8,128)S(1)} %all_gather.3), channel_id=1, source_target_pairs={{0,4},{4,8},{8,12},{12,16},{16,20},{20,24},{24,28},{28,32},{32,36}... | collective-permute-start | bytes 147464 | tf_op jit(solution)/shard_map/ppermute | solution.py:17
  20.6 1.6 %convert_reduce_fusion = f32[512,128]{1,0:T(8,128)} fusion(s32[8,128]{1,0:T(8,128)} %param.19), kind=kLoop, calls=%fused_computation.3 | loop fusion | flops 1507328 | bytes 266240 | tf_op jit(solution)/shard_map/reduce_sum | solution.py:88
  23.8 1.6 %copy.35 = bf16[6,24,128]{1,0,2:T(8,128)(2,1)} copy(bf16[6,24,128]{2,1,0:T(8,128)(2,1)} %param.17) | data formatting | bytes 73728 | tf_op args[6]
  25.4 1.3 %copy.29 = f32[512,3,128]{2,1,0:T(4,128)S(1)} copy(bf16[512,3,128]{2,0,1:T(8,128)(2,1)} %param.14) | data formatting | bytes 1179648 | tf_op jit(solution)/shard_map/convert_element_type | solution.py:70
  26.8 1.2 %reshape.111 = f32[1536,128]{1,0:T(8,128)} reshape(f32[512,3,128]{2,1,0:T(4,128)S(1)} %copy.29) | data formatting | bytes 1572864 | tf_op jit(solution)/shard_map/convert_element_type | solution.py:70
  28.0 1.4 %copy.30 = f32[1536,128]{0,1:T(8,128)S(1)} copy(f32[1536,128]{1,0:T(8,128)} %reshape.111) | data formatting | bytes 1572864 | tf_op jit(solution)/shard_map/convert_element_type | solution.py:70
  31.1 3.9 %gather_fusion = bf16[1024,384]{1,0:T(8,128)(2,1)S(1)} fusion(bf16[512,384]{1,0:T(8,128)(2,1)S(1)} %reshape.106, s32[1024]{0:T(1024)S(1)} %broadcast_clamp_fusion), kind=kCustom, calls=%fused_computation | custom fusion | bytes 1576960 | tf_op jit(solution)/shard_map/gather | solution.py:81
  35.5 1.3 %convolution_bitcast_fusion.1 = f32[128,6,128]{2,1,0:T(8,128)S(1)} fusion(bf16[128,24,128]{2,1,0:T(8,128)(2,1)S(1)} %reshape.107, bf16[6,24,128]{1,0,2:T(8,128)(2,1)} %copy.35), kind=kOutput, calls=%fused_computation.10 | convolution fusion | flops 4718592 | bytes 1216512 | tf_op jit(solution)/shard_map/ije,ejl->eil/dot_general | solution.py:82
  37.6 2.3 %fusion.37 = f32[512,768]{1,0:T(8,128)S(1)} fusion(f32[512,128]{1,0:T(8,128)} %convert_reduce_fusion, f32[128,768]{0,1:T(8,128)S(1)} %bitcast.76), kind=kOutput, calls=%fused_computation.75 | convolution fusion | flops 603979776 | bytes 2228224 | tf_op jit(solution)/shard_map/dot_general | solution.py:91
  41.0 2.4 %collective-permute-start.6 = (f32[1,2,8,6,128]{4,2,3,1,0:T(8,128)S(1)}, f32[1,2,8,6,128]{4,2,3,1,0:T(8,128)S(1)}, u32[]{:S(2)}, u32[]{:S(2)}) collective-permute-start(f32[1,2,8,6,128]{4,2,3,1,0:T(8,128)S(1)} %get-tuple-element.12), channel_id=1, source_target_pairs={{0,4},{4,8},{8,12},{12,16},{16,20},{20,24},{24,28},{28,32},{32,36}... | collective-permute-start | bytes 147464 | tf_op jit(solution)/shard_map/ppermute | solution.py:17
  43.4 1.9 %collective-permute-start.7 = (f32[1,2,8,6,128]{4,2,3,1,0:T(8,128)S(1)}, f32[1,2,8,6,128]{4,2,3,1,0:T(8,128)S(1)}, u32[]{:S(2)}, u32[]{:S(2)}) collective-permute-start(f32[1,2,8,6,128]{4,2,3,1,0:T(8,128)S(1)} %get-tuple-element.13), channel_id=1, source_target_pairs={{4,0},{8,4},{12,8},{16,12},{20,16},{24,20},{28,24},{32,28},{36,32}... | collective-permute-start | bytes 147464 | tf_op jit(solution)/shard_map/ppermute | solution.py:20
  45.3 6.8 %collective-permute-done.7 = f32[1,2,8,6,128]{4,2,3,1,0:T(8,128)S(1)} collective-permute-done((f32[1,2,8,6,128]{4,2,3,1,0:T(8,128)S(1)}, f32[1,2,8,6,128]{4,2,3,1,0:T(8,128)S(1)}, u32[]{:S(2)}, u32[]{:S(2)}) %collective-permute-start.7) | collective-permute-done | bytes 49184 | tf_op jit(solution)/shard_map/ppermute | solution.py:20
  52.2 1.9 %collective-permute-start.8 = (f32[4,1,8,6,128]{4,2,3,1,0:T(8,128)S(1)}, f32[4,1,8,6,128]{4,2,3,1,0:T(8,128)S(1)}, u32[]{:S(2)}, u32[]{:S(2)}) collective-permute-start(f32[4,1,8,6,128]{4,2,3,1,0:T(8,128)S(1)} %get-tuple-element.14), channel_id=1, source_target_pairs={{0,1},{1,2},{2,3},{4,5},{5,6},{6,7},{8,9},{9,10},{10,11},{12,13},{... | collective-permute-start | bytes 294920 | tf_op jit(solution)/shard_map/ppermute | solution.py:17
  54.1 3.4 %collective-permute-start.9 = (f32[4,1,8,6,128]{4,2,3,1,0:T(8,128)S(1)}, f32[4,1,8,6,128]{4,2,3,1,0:T(8,128)S(1)}, u32[]{:S(2)}, u32[]{:S(2)}) collective-permute-start(f32[4,1,8,6,128]{4,2,3,1,0:T(8,128)S(1)} %get-tuple-element.15), channel_id=1, source_target_pairs={{1,0},{2,1},{3,2},{5,4},{6,5},{7,6},{9,8},{10,9},{11,10},{13,12},{... | collective-permute-start | bytes 294920 | tf_op jit(solution)/shard_map/ppermute | solution.py:20
  57.5 2.5 %collective-permute-done.9 = f32[4,1,8,6,128]{4,2,3,1,0:T(8,128)S(1)} collective-permute-done((f32[4,1,8,6,128]{4,2,3,1,0:T(8,128)S(1)}, f32[4,1,8,6,128]{4,2,3,1,0:T(8,128)S(1)}, u32[]{:S(2)}, u32[]{:S(2)}) %collective-permute-start.9) | collective-permute-done | bytes 98336 | tf_op jit(solution)/shard_map/ppermute | solution.py:20
  60.8 1.6 %slice.85 = f32[1,32,6,128]{3,2,1,0:T(8,128)} reshape(f32[32,768]{1,0:T(8,128)} %get-tuple-element.9) | data formatting | bytes 196608 | tf_op jit(solution)/shard_map/slice | solution.py:18
  63.1 2.7 %collective-permute-start.5 = (f32[1,32,6,128]{3,2,1,0:T(8,128)}, f32[1,32,6,128]{3,2,1,0:T(8,128)S(1)}, u32[]{:S(2)}, u32[]{:S(2)}) collective-permute-start(f32[1,32,6,128]{3,2,1,0:T(8,128)} %slice.87), channel_id=1, source_target_pairs={{1,0},{2,1},{3,2},{5,4},{6,5},{7,6},{9,8},{10,9},{11,10},{13,12},{... | collective-permute-start | bytes 294920 | tf_op jit(solution)/shard_map/ppermute | solution.py:20
  65.8 2.5 %collective-permute-start.4 = (f32[1,32,6,128]{3,2,1,0:T(8,128)}, f32[1,32,6,128]{3,2,1,0:T(8,128)S(1)}, u32[]{:S(2)}, u32[]{:S(2)}) collective-permute-start(f32[1,32,6,128]{3,2,1,0:T(8,128)} %slice.85), channel_id=1, source_target_pairs={{0,1},{1,2},{2,3},{4,5},{5,6},{6,7},{8,9},{9,10},{10,11},{12,13},{... | collective-permute-start | bytes 294920 | tf_op jit(solution)/shard_map/ppermute | solution.py:17
  69.2 2.6 %collective-permute-done.4 = f32[1,32,6,128]{3,2,1,0:T(8,128)S(1)} collective-permute-done((f32[1,32,6,128]{3,2,1,0:T(8,128)}, f32[1,32,6,128]{3,2,1,0:T(8,128)S(1)}, u32[]{:S(2)}, u32[]{:S(2)}) %collective-permute-start.4) | collective-permute-done | bytes 98336 | tf_op jit(solution)/shard_map/ppermute | solution.py:17
  72.6 1.7 %slice.80 = f32[1,64,6,128]{3,2,1,0:T(8,128)} reshape(f32[64,768]{1,0:T(8,128)} %get-tuple-element.6) | data formatting | bytes 393216 | tf_op jit(solution)/shard_map/slice | solution.py:18
  74.3 1.7 %slice.82 = f32[1,64,6,128]{3,2,1,0:T(8,128)} reshape(f32[64,768]{1,0:T(8,128)} %get-tuple-element.8) | data formatting | bytes 393216 | tf_op jit(solution)/shard_map/slice | solution.py:20
  76.0 1.9 %collective-permute-start.3 = (f32[1,64,6,128]{3,2,1,0:T(8,128)}, f32[1,64,6,128]{3,2,1,0:T(8,128)}, u32[]{:S(2)}, u32[]{:S(2)}) collective-permute-start(f32[1,64,6,128]{3,2,1,0:T(8,128)} %slice.82), channel_id=1, source_target_pairs={{4,0},{8,4},{12,8},{16,12},{20,16},{24,20},{28,24},{32,28},{36,32}... | collective-permute-start | bytes 589832 | tf_op jit(solution)/shard_map/ppermute | solution.py:20
  77.9 7.0 %collective-permute-start.2 = (f32[1,64,6,128]{3,2,1,0:T(8,128)}, f32[1,64,6,128]{3,2,1,0:T(8,128)}, u32[]{:S(2)}, u32[]{:S(2)}) collective-permute-start(f32[1,64,6,128]{3,2,1,0:T(8,128)} %slice.80), channel_id=1, source_target_pairs={{0,4},{4,8},{8,12},{12,16},{16,20},{20,24},{24,28},{28,32},{32,36}... | collective-permute-start | bytes 589832 | tf_op jit(solution)/shard_map/ppermute | solution.py:17
  84.9 2.1 %reshape_reshape.3 = bf16[512,3,128]{2,1,0:T(4,128)(2,1)} reshape(bf16[4,384,128]{2,1,0:T(8,128)(2,1)} %copy-done.1) | data formatting | bytes 786432 | tf_op jit(solution)/shard_map/reshape;reshape | solution.py:130
  87.0 1.6 %copy.39 = f32[512,768]{0,1:T(8,128)} copy(f32[512,768]{1,0:T(8,128)S(1)} %fusion.37) | data formatting | bytes 3145728 | tf_op jit(solution)/shard_map/dot_general | solution.py:91
  88.6 1.8 %copy.41 = bf16[512,3,128]{2,0,1:T(8,128)(2,1)} copy(bf16[512,3,128]{2,1,0:T(4,128)(2,1)} %reshape_reshape.3) | data formatting | bytes 786432
  90.5 1.9 %copy.40 = f32[512,6,128]{2,0,1:T(8,128)S(1)} copy(f32[512,6,128]{0,2,1:T(8,128)} %bitcast.74) | data formatting | bytes 3145728 | tf_op jit(solution)/shard_map/reshape | solution.py:93
  92.4 1.1 %pad_maximum_fusion = f32[2,64,6,128]{3,2,1,0:T(8,128)S(1)} fusion(f32[1,64,6,128]{3,2,1,0:T(8,128)} %collective-permute-done.3, f32[1,64,6,128]{3,2,1,0:T(8,128)} %collective-permute-done.2), kind=kLoop, calls=%fused_computation.15 | loop fusion | flops 98304 | bytes 786432 | tf_op jit(solution)/shard_map/stack | solution.py:102
  93.7 1.2 %copy.37 = f32[768,224]{1,0:T(8,128)} copy(f32[768,224]{0,1:T(8,128)S(1)} %maximum_bitcast_fusion) | data formatting | bytes 1376256 | tf_op jit(solution)/shard_map/dot_general | solution.py:124
  94.9 3.2 %divide_convert_fusion = bf16[512,6,128]{2,0,1:T(8,128)(2,1)} fusion(f32[512,6,128]{2,0,1:T(8,128)S(1)} %copy.40, f32[6,128,224]{2,1,0:T(8,128)} %bitcast.78, f32[512]{0:T(512)S(1)} %copy-done.7, pred[512]{0:T(512)(128)(4,1)S(1)} %broadcast_compare_fusion, s32[224]{0:T(256)S(1)} %bitcast.86), kind=kOutput, calls=%fused_computation.5 | convolution fusion | flops 1058373632 | bytes 3050880 | tf_op jit(solution)/shard_map/dot_general | solution.py:124
  (61 shorter events, 9.5 us)
Async XLA Ops:
  0.6 29.6 %copy-start = (bf16[4,384,384]{2,1,0:T(8,128)(2,1)S(1)}, bf16[4,384,384]{2,1,0:T(8,128)(2,1)}, u32[]{:S(2)}) copy-start(bf16[4,384,384]{2,1,0:T(8,128)(2,1)} %param.15) | copy-start | bytes 3538948
  10.1 19.3 %collective-permute-start.1 = (f32[96,128]{1,0:T(8,128)S(1)}, f32[96,128]{1,0:T(8,128)S(1)}, u32[]{:S(2)}, u32[]{:S(2)}) collective-permute-start(f32[96,128]{1,0:T(8,128)S(1)} %all_gather.3), channel_id=1, source_target_pairs={{4,0},{8,4},{12,8},{16,12},{20,16},{24,20},{28,24},{32,28},{36,32}... | collective-permute-start | bytes 147464 | tf_op jit(solution)/shard_map/ppermute | solution.py:20
  15.5 13.9 %collective-permute-start = (f32[96,128]{1,0:T(8,128)S(1)}, f32[96,128]{1,0:T(8,128)S(1)}, u32[]{:S(2)}, u32[]{:S(2)}) collective-permute-start(f32[96,128]{1,0:T(8,128)S(1)} %all_gather.3), channel_id=1, source_target_pairs={{0,4},{4,8},{8,12},{12,16},{16,20},{20,24},{24,28},{28,32},{32,36}... | collective-permute-start | bytes 147464 | tf_op jit(solution)/shard_map/ppermute | solution.py:17
  26.8 2.9 %copy-start.4 = (bf16[1536,24]{0,1:T(8,128)(2,1)S(1)}, bf16[1536,24]{0,1:T(8,128)(2,1)}, u32[]{:S(2)}) copy-start(bf16[1536,24]{0,1:T(8,128)(2,1)} %param.13) | copy-start | bytes 221188
  30.9 4.1 %copy-start.1 = (bf16[4,384,128]{2,1,0:T(8,128)(2,1)}, bf16[4,384,128]{2,1,0:T(8,128)(2,1)S(1)}, u32[]{:S(2)}) copy-start(bf16[4,384,128]{2,1,0:T(8,128)(2,1)S(1)} %copy.32) | copy-start | bytes 1179652
  35.1 1.7 %copy-start.6 = (f32[128]{0:T(128)S(1)}, f32[128]{0:T(128)}, u32[]{:S(2)}) copy-start(f32[128]{0:T(128)} %param.18) | copy-start | bytes 1540
  37.4 2.6 %copy-start.5 = (s32[1,224]{1,0:T(1,128)S(1)}, s32[1,224]{1,0:T(1,128)}, u32[]{:S(2)}) copy-start(s32[1,224]{1,0:T(1,128)} %param.20) | copy-start | bytes 2692
  41.0 4.4 %collective-permute-start.6 = (f32[1,2,8,6,128]{4,2,3,1,0:T(8,128)S(1)}, f32[1,2,8,6,128]{4,2,3,1,0:T(8,128)S(1)}, u32[]{:S(2)}, u32[]{:S(2)}) collective-permute-start(f32[1,2,8,6,128]{4,2,3,1,0:T(8,128)S(1)} %get-tuple-element.12), channel_id=1, source_target_pairs={{0,4},{4,8},{8,12},{12,16},{16,20},{20,24},{24,28},{28,32},{32,36}... | collective-permute-start | bytes 147464 | tf_op jit(solution)/shard_map/ppermute | solution.py:17
  43.4 8.7 %collective-permute-start.7 = (f32[1,2,8,6,128]{4,2,3,1,0:T(8,128)S(1)}, f32[1,2,8,6,128]{4,2,3,1,0:T(8,128)S(1)}, u32[]{:S(2)}, u32[]{:S(2)}) collective-permute-start(f32[1,2,8,6,128]{4,2,3,1,0:T(8,128)S(1)} %get-tuple-element.13), channel_id=1, source_target_pairs={{4,0},{8,4},{12,8},{16,12},{20,16},{24,20},{28,24},{32,28},{36,32}... | collective-permute-start | bytes 147464 | tf_op jit(solution)/shard_map/ppermute | solution.py:20
  52.2 5.4 %collective-permute-start.8 = (f32[4,1,8,6,128]{4,2,3,1,0:T(8,128)S(1)}, f32[4,1,8,6,128]{4,2,3,1,0:T(8,128)S(1)}, u32[]{:S(2)}, u32[]{:S(2)}) collective-permute-start(f32[4,1,8,6,128]{4,2,3,1,0:T(8,128)S(1)} %get-tuple-element.14), channel_id=1, source_target_pairs={{0,1},{1,2},{2,3},{4,5},{5,6},{6,7},{8,9},{9,10},{10,11},{12,13},{... | collective-permute-start | bytes 294920 | tf_op jit(solution)/shard_map/ppermute | solution.py:17
  54.1 6.0 %collective-permute-start.9 = (f32[4,1,8,6,128]{4,2,3,1,0:T(8,128)S(1)}, f32[4,1,8,6,128]{4,2,3,1,0:T(8,128)S(1)}, u32[]{:S(2)}, u32[]{:S(2)}) collective-permute-start(f32[4,1,8,6,128]{4,2,3,1,0:T(8,128)S(1)} %get-tuple-element.15), channel_id=1, source_target_pairs={{1,0},{2,1},{3,2},{5,4},{6,5},{7,6},{9,8},{10,9},{11,10},{13,12},{... | collective-permute-start | bytes 294920 | tf_op jit(solution)/shard_map/ppermute | solution.py:20
  63.1 6.1 %collective-permute-start.5 = (f32[1,32,6,128]{3,2,1,0:T(8,128)}, f32[1,32,6,128]{3,2,1,0:T(8,128)S(1)}, u32[]{:S(2)}, u32[]{:S(2)}) collective-permute-start(f32[1,32,6,128]{3,2,1,0:T(8,128)} %slice.87), channel_id=1, source_target_pairs={{1,0},{2,1},{3,2},{5,4},{6,5},{7,6},{9,8},{10,9},{11,10},{13,12},{... | collective-permute-start | bytes 294920 | tf_op jit(solution)/shard_map/ppermute | solution.py:20
  65.8 5.9 %collective-permute-start.4 = (f32[1,32,6,128]{3,2,1,0:T(8,128)}, f32[1,32,6,128]{3,2,1,0:T(8,128)S(1)}, u32[]{:S(2)}, u32[]{:S(2)}) collective-permute-start(f32[1,32,6,128]{3,2,1,0:T(8,128)} %slice.85), channel_id=1, source_target_pairs={{0,1},{1,2},{2,3},{4,5},{5,6},{6,7},{8,9},{9,10},{10,11},{12,13},{... | collective-permute-start | bytes 294920 | tf_op jit(solution)/shard_map/ppermute | solution.py:17
  76.0 16.4 %collective-permute-start.3 = (f32[1,64,6,128]{3,2,1,0:T(8,128)}, f32[1,64,6,128]{3,2,1,0:T(8,128)}, u32[]{:S(2)}, u32[]{:S(2)}) collective-permute-start(f32[1,64,6,128]{3,2,1,0:T(8,128)} %slice.82), channel_id=1, source_target_pairs={{4,0},{8,4},{12,8},{16,12},{20,16},{24,20},{28,24},{32,28},{36,32}... | collective-permute-start | bytes 589832 | tf_op jit(solution)/shard_map/ppermute | solution.py:20
  77.9 14.5 %collective-permute-start.2 = (f32[1,64,6,128]{3,2,1,0:T(8,128)}, f32[1,64,6,128]{3,2,1,0:T(8,128)}, u32[]{:S(2)}, u32[]{:S(2)}) collective-permute-start(f32[1,64,6,128]{3,2,1,0:T(8,128)} %slice.80), channel_id=1, source_target_pairs={{0,4},{4,8},{8,12},{12,16},{16,20},{20,24},{24,28},{28,32},{32,36}... | collective-permute-start | bytes 589832 | tf_op jit(solution)/shard_map/ppermute | solution.py:17
  92.3 1.3 %copy-start.2 = (f32[64,768]{1,0:T(8,128)S(1)}, f32[64,768]{1,0:T(8,128)}, u32[]{:S(2)}) copy-start(f32[64,768]{1,0:T(8,128)} %get-tuple-element.7) | copy-start | bytes 589828
  92.3 1.3 %copy-start.3 = (f32[32,768]{1,0:T(8,128)S(1)}, f32[32,768]{1,0:T(8,128)}, u32[]{:S(2)}) copy-start(f32[32,768]{1,0:T(8,128)} %get-tuple-element.10) | copy-start | bytes 294916
  93.6 1.2 %copy-start.7 = (f32[512]{0:T(512)S(1)}, f32[512]{0:T(512)}, u32[]{:S(2)}) copy-start(f32[512]{0:T(512)} %param.21) | copy-start | bytes 6148
where the time goes:
time: 98.9 us; the launch traced here: 98 us
  starting transfers between devices  33.5 us (34%)
  local copies, waits for them, and re-layouts  24.9 us (25%)
  waiting for transfers between devices  12.6 us (13%)
  matrix products  9.65 us (10%)
  blocking collectives  9.42 us (10%)
  other arithmetic  6.77 us (7%)
  between operations  1.1 us (1%)
    ppermute x5, starting transfers between devices, padded(): lax.ppermute(lax.slice_in_dim(block, block.shape[dim] - width, None, axis...  18.1 us
    ppermute x5, starting transfers between devices, padded(): lax.ppermute(lax.slice_in_dim(block, 0, width, axis=dim), axis, backward)  15.4 us
    ppermute x5, waiting for transfers between devices, padded(): lax.ppermute(lax.slice_in_dim(block, 0, width, axis=dim), axis, backward)  9.97 us
    all_gather x1, blocking collectives, shards(): group_rows = lax.all_gather(coarse, 'grp', axis=0, tiled=True)  9.42 us
    convert_element_type x3, local copies, waits for them, and re-layouts, shards(): force.reshape(3 * node_count, load_cases).astype(jnp.float32) - correction  3.97 us
    gather x1, local copies, waits for them, and re-layouts, shards(): element = displaced[connect.T].reshape(elem_count, 24, load_cases)  3.92 us
    unnamed x18, local copies, waits for them, and re-layouts  3.52 us
    slice x4, local copies, waits for them, and re-layouts, padded(): lax.slice_in_dim(block, block.shape[dim] - width, None, axis=dim)  3.25 us
  transfers between devices with their start and end apart: 10, of which 4 were waited for; matrix products, arithmetic and copies ran while one was open for 17% of the time, Pallas kernels for 0%

commit v1 on v0

--- a/solution.py
+++ b/solution.py
@@ -52,7 +52,19 @@
     interface,
     nodal_volume,
 ):
-    group_rows = lax.all_gather(coarse, "grp", axis=0, tiled=True)
+    n_parts = lax.axis_size("grp")
+    shelf = [(rr, (rr + 1) % n_parts) for rr in range(n_parts)]
+    made = [(rr, (rr - 1) % n_parts) for rr in range(n_parts)]
+    step_out, v1 = ([coarse], [coarse])
+    for _ in range(n_parts // 2):
+        carry_out = lax.ppermute(step_out[-1], "grp", shelf)
+        step_out.append(carry_out)
+    for _ in [*range((n_parts - 1) // 2)]:
+        latest = lax.ppermute(v1[-1], "grp", made)
+        v1.append(latest)
+    small = jnp.concatenate([*step_out[::-1], *v1[1:]], 0)
+    val2 = lax.axis_index("grp")
+    group_rows = jnp.roll(small, (val2 - n_parts // 2) * coarse.shape[0], 0)
     block_rows = group_rows.shape[0]
     nearby = padded(group_rows, (("sub", 0),), block_rows)
     offset = (lax.axis_index("sub") - 1) * block_rows

time: 98.9 us -> 93.9 us (0.949)
  blocking collectives: 9.42 us -> 0 us
  starting transfers between devices: 33.5 us -> 39.2 us
    all_gather x1 -> x0, blocking collectives: 9.42 us -> none  [shards(): group_rows = lax.all_gather(coarse, 'grp', axis=0, tiled=True)]
    ppermute x5, starting transfers between devices: 18.1 us -> 23.1 us  [padded(): lax.ppermute(lax.slice_in_dim(block, block.shape[dim] - width, None, axis...]
    ppermute x0 -> x3, starting transfers between devices: none -> 2.75 us  [the longest x2 2.5 us: shards(): carry_out = lax.ppermute(step_out[-1], 'grp', shelf)]
    ppermute x5, starting transfers between devices: 15.4 us -> 13.3 us  [padded(): lax.ppermute(lax.slice_in_dim(block, 0, width, axis=dim), axis, backward)]
    convert_element_type x3, local copies, waits for them, and re-layouts: 3.97 us -> 1.96 us  [shards(): force.reshape(3 * node_count, load_cases).astype(jnp.float32) - correction]
    unnamed x18 -> x25, local copies, waits for them, and re-layouts: 3.52 us -> 4.28 us
  transfers between devices with their start and end apart: 10 -> 13, of which waited for: 4 -> 4; matrix products, arithmetic and copies ran while one was open for 17% -> 16% of each run, Pallas kernels for 0% -> 0%
where the time goes in v1:
time: 93.9 us; the launch traced here: 93 us
  starting transfers between devices  39.2 us (42%)
  local copies, waits for them, and re-layouts  24.4 us (26%)
  waiting for transfers between devices  12.6 us (13%)
  matrix products  8.83 us (9%)
  other arithmetic  6.78 us (7%)
  between operations  1.12 us (1%)
    ppermute x5, starting transfers between devices, padded(): lax.ppermute(lax.slice_in_dim(block, block.shape[dim] - width, None, axis...  23.1 us
    ppermute x5, starting transfers between devices, padded(): lax.ppermute(lax.slice_in_dim(block, 0, width, axis=dim), axis, backward)  13.3 us
    ppermute x5, waiting for transfers between devices, padded(): lax.ppermute(lax.slice_in_dim(block, 0, width, axis=dim), axis, backward)  9.81 us
    unnamed x25, local copies, waits for them, and re-layouts  4.28 us
    gather x1, local copies, waits for them, and re-layouts, shards(): element = displaced[connect.T].reshape(elem_count, 24, load_cases)  3.92 us
    slice x4, local copies, waits for them, and re-layouts, padded(): lax.slice_in_dim(block, block.shape[dim] - width, None, axis=dim)  3.24 us
    dot_general x1, matrix products, shards(): jnp.dot(picker.T, summed_rows.reshape(-1, 6 * load_cases), precision=lax....  3.18 us
    ppermute x5, waiting for transfers between devices, padded(): lax.ppermute(lax.slice_in_dim(block, block.shape[dim] - width, None, axis...  2.81 us
  transfers between devices with their start and end apart: 13, of which 4 were waited for; matrix products, arithmetic and copies ran while one was open for 16% of the time, Pallas kernels for 0%

profile of v1, /device:TPU:123, one launch (start us, length us, event | category | flops | bytes accessed | tf_op | source)
XLA Modules:
  0.0 93.0 jit_solution(7339419901326776894)
XLA Ops:
  0.6 1.3 %collective-permute-start = (f32[24,128]{1,0:T(8,128)}, f32[24,128]{1,0:T(8,128)S(1)}, u32[]{:S(2)}, u32[]{:S(2)}) collective-permute-start(f32[24,128]{1,0:T(8,128)} %param.11), channel_id=1, source_target_pairs={{0,1},{1,2},{2,3},{3,0},{4,5},{5,6},{6,7},{7,4},{8,9},{9,10},{10,1... | collective-permute-start | bytes 36872 | tf_op jit(solution)/shard_map/ppermute | solution.py:60
  4.5 1.2 %collective-permute-start.1 = (f32[24,128]{1,0:T(8,128)S(1)}, f32[24,128]{1,0:T(8,128)S(1)}, u32[]{:S(2)}, u32[]{:S(2)}) collective-permute-start(f32[24,128]{1,0:T(8,128)S(1)} %collective-permute-done), channel_id=1, source_target_pairs={{0,1},{1,2},{2,3},{3,0},{4,5},{5,6},{6,7},{7,4},{8,9},{9,10},{10,1... | collective-permute-start | bytes 36872 | tf_op jit(solution)/shard_map/ppermute | solution.py:60
  5.7 1.6 %convert_reduce_fusion = f32[512,128]{1,0:T(8,128)} fusion(s32[8,128]{1,0:T(8,128)} %param.19), kind=kLoop, calls=%fused_computation.3 | loop fusion | flops 1507328 | bytes 266240 | tf_op jit(solution)/shard_map/reduce_sum | solution.py:100
  8.8 4.0 %collective-permute-start.4 = (f32[96,128]{1,0:T(8,128)S(1)}, f32[96,128]{1,0:T(8,128)S(1)}, u32[]{:S(2)}, u32[]{:S(2)}) collective-permute-start(f32[96,128]{1,0:T(8,128)S(1)} %constant_dynamic-slice_fusion), channel_id=1, source_target_pairs={{4,0},{8,4},{12,8},{16,12},{20,16},{24,20},{28,24},{32,28},{36,32}... | collective-permute-start | bytes 147464 | tf_op jit(solution)/shard_map/ppermute | solution.py:20
  12.8 4.9 %collective-permute-start.3 = (f32[96,128]{1,0:T(8,128)S(1)}, f32[96,128]{1,0:T(8,128)S(1)}, u32[]{:S(2)}, u32[]{:S(2)}) collective-permute-start(f32[96,128]{1,0:T(8,128)S(1)} %constant_dynamic-slice_fusion), channel_id=1, source_target_pairs={{0,4},{4,8},{8,12},{12,16},{16,20},{20,24},{24,28},{28,32},{32,36}... | collective-permute-start | bytes 147464 | tf_op jit(solution)/shard_map/ppermute | solution.py:17
  17.7 1.0 %copy.35 = bf16[6,24,128]{1,0,2:T(8,128)(2,1)S(1)} copy(bf16[6,24,128]{2,1,0:T(8,128)(2,1)} %param.17) | data formatting | bytes 73728 | tf_op args[6]
  18.7 1.3 %copy.29 = f32[512,3,128]{2,1,0:T(4,128)S(1)} copy(bf16[512,3,128]{2,0,1:T(8,128)(2,1)} %param.14) | data formatting | bytes 1179648 | tf_op jit(solution)/shard_map/convert_element_type | solution.py:82
  22.4 3.9 %gather_fusion = bf16[1024,384]{1,0:T(8,128)(2,1)S(1)} fusion(bf16[512,384]{1,0:T(8,128)(2,1)S(1)} %reshape.106, s32[1024]{0:T(1024)S(1)} %broadcast_clamp_fusion), kind=kCustom, calls=%fused_computation | custom fusion | bytes 1576960 | tf_op jit(solution)/shard_map/gather | solution.py:93
  27.7 1.0 %copy.36 = f32[128,6,128]{0,2,1:T(8,128)} copy(f32[128,6,128]{2,1,0:T(8,128)S(1)} %fusion.2) | data formatting | bytes 786432 | tf_op jit(solution)/shard_map/mul | solution.py:96
  28.7 2.5 %fusion.37 = f32[512,768]{1,0:T(8,128)S(1)} fusion(f32[512,128]{1,0:T(8,128)} %convert_reduce_fusion, f32[128,768]{0,1:T(8,128)} %bitcast.76), kind=kOutput, calls=%fused_computation.84 | convolution fusion | flops 603979776 | bytes 2228224 | tf_op jit(solution)/shard_map/dot_general | solution.py:103
  31.2 0.9 %fusion.6 = f32[224,768]{1,0:T(8,128)S(1)} fusion(f32[512,768]{1,0:T(8,128)S(1)} %fusion.37, s32[224]{0:T(256)S(1)} %bitcast.84), kind=kOutput, calls=%fused_computation.19 | convolution fusion | flops 1057079296 | bytes 2261888 | tf_op jit(solution)/shard_map/dot_general | solution.py:108
  32.1 5.7 %collective-permute-start.9 = (f32[1,2,8,6,128]{4,2,3,1,0:T(8,128)S(1)}, f32[1,2,8,6,128]{4,2,3,1,0:T(8,128)S(1)}, u32[]{:S(2)}, u32[]{:S(2)}) collective-permute-start(f32[1,2,8,6,128]{4,2,3,1,0:T(8,128)S(1)} %get-tuple-element.12), channel_id=1, source_target_pairs={{0,4},{4,8},{8,12},{12,16},{16,20},{20,24},{24,28},{28,32},{32,36}... | collective-permute-start | bytes 147464 | tf_op jit(solution)/shard_map/ppermute | solution.py:17
  37.9 1.9 %collective-permute-start.10 = (f32[1,2,8,6,128]{4,2,3,1,0:T(8,128)S(1)}, f32[1,2,8,6,128]{4,2,3,1,0:T(8,128)S(1)}, u32[]{:S(2)}, u32[]{:S(2)}) collective-permute-start(f32[1,2,8,6,128]{4,2,3,1,0:T(8,128)S(1)} %get-tuple-element.13), channel_id=1, source_target_pairs={{4,0},{8,4},{12,8},{16,12},{20,16},{24,20},{28,24},{32,28},{36,32}... | collective-permute-start | bytes 147464 | tf_op jit(solution)/shard_map/ppermute | solution.py:20
  39.8 6.8 %collective-permute-done.10 = f32[1,2,8,6,128]{4,2,3,1,0:T(8,128)S(1)} collective-permute-done((f32[1,2,8,6,128]{4,2,3,1,0:T(8,128)S(1)}, f32[1,2,8,6,128]{4,2,3,1,0:T(8,128)S(1)}, u32[]{:S(2)}, u32[]{:S(2)}) %collective-permute-start.10) | collective-permute-done | bytes 49184 | tf_op jit(solution)/shard_map/ppermute | solution.py:20
  46.7 2.8 %collective-permute-start.11 = (f32[4,1,8,6,128]{4,2,3,1,0:T(8,128)S(1)}, f32[4,1,8,6,128]{4,2,3,1,0:T(8,128)S(1)}, u32[]{:S(2)}, u32[]{:S(2)}) collective-permute-start(f32[4,1,8,6,128]{4,2,3,1,0:T(8,128)S(1)} %get-tuple-element.14), channel_id=1, source_target_pairs={{0,1},{1,2},{2,3},{4,5},{5,6},{6,7},{8,9},{9,10},{10,11},{12,13},{... | collective-permute-start | bytes 294920 | tf_op jit(solution)/shard_map/ppermute | solution.py:17
  49.5 2.8 %collective-permute-start.12 = (f32[4,1,8,6,128]{4,2,3,1,0:T(8,128)S(1)}, f32[4,1,8,6,128]{4,2,3,1,0:T(8,128)S(1)}, u32[]{:S(2)}, u32[]{:S(2)}) collective-permute-start(f32[4,1,8,6,128]{4,2,3,1,0:T(8,128)S(1)} %get-tuple-element.15), channel_id=1, source_target_pairs={{1,0},{2,1},{3,2},{5,4},{6,5},{7,6},{9,8},{10,9},{11,10},{13,12},{... | collective-permute-start | bytes 294920 | tf_op jit(solution)/shard_map/ppermute | solution.py:20
  52.3 2.5 %collective-permute-done.12 = f32[4,1,8,6,128]{4,2,3,1,0:T(8,128)S(1)} collective-permute-done((f32[4,1,8,6,128]{4,2,3,1,0:T(8,128)S(1)}, f32[4,1,8,6,128]{4,2,3,1,0:T(8,128)S(1)}, u32[]{:S(2)}, u32[]{:S(2)}) %collective-permute-start.12) | collective-permute-done | bytes 98336 | tf_op jit(solution)/shard_map/ppermute | solution.py:20
  55.7 1.6 %slice.85 = f32[1,32,6,128]{3,2,1,0:T(8,128)} reshape(f32[32,768]{1,0:T(8,128)} %get-tuple-element.9) | data formatting | bytes 196608 | tf_op jit(solution)/shard_map/slice | solution.py:18
  57.9 2.7 %collective-permute-start.8 = (f32[1,32,6,128]{3,2,1,0:T(8,128)}, f32[1,32,6,128]{3,2,1,0:T(8,128)S(1)}, u32[]{:S(2)}, u32[]{:S(2)}) collective-permute-start(f32[1,32,6,128]{3,2,1,0:T(8,128)} %slice.87), channel_id=1, source_target_pairs={{1,0},{2,1},{3,2},{5,4},{6,5},{7,6},{9,8},{10,9},{11,10},{13,12},{... | collective-permute-start | bytes 294920 | tf_op jit(solution)/shard_map/ppermute | solution.py:20
  60.6 2.5 %collective-permute-start.7 = (f32[1,32,6,128]{3,2,1,0:T(8,128)}, f32[1,32,6,128]{3,2,1,0:T(8,128)S(1)}, u32[]{:S(2)}, u32[]{:S(2)}) collective-permute-start(f32[1,32,6,128]{3,2,1,0:T(8,128)} %slice.85), channel_id=1, source_target_pairs={{0,1},{1,2},{2,3},{4,5},{5,6},{6,7},{8,9},{9,10},{10,11},{12,13},{... | collective-permute-start | bytes 294920 | tf_op jit(solution)/shard_map/ppermute | solution.py:17
  63.8 2.8 %collective-permute-done.7 = f32[1,32,6,128]{3,2,1,0:T(8,128)S(1)} collective-permute-done((f32[1,32,6,128]{3,2,1,0:T(8,128)}, f32[1,32,6,128]{3,2,1,0:T(8,128)S(1)}, u32[]{:S(2)}, u32[]{:S(2)}) %collective-permute-start.7) | collective-permute-done | bytes 98336 | tf_op jit(solution)/shard_map/ppermute | solution.py:17
  67.4 1.7 %slice.80 = f32[1,64,6,128]{3,2,1,0:T(8,128)} reshape(f32[64,768]{1,0:T(8,128)} %get-tuple-element.6) | data formatting | bytes 393216 | tf_op jit(solution)/shard_map/slice | solution.py:18
  69.1 1.7 %slice.82 = f32[1,64,6,128]{3,2,1,0:T(8,128)} reshape(f32[64,768]{1,0:T(8,128)} %get-tuple-element.8) | data formatting | bytes 393216 | tf_op jit(solution)/shard_map/slice | solution.py:20
  70.7 1.9 %collective-permute-start.6 = (f32[1,64,6,128]{3,2,1,0:T(8,128)}, f32[1,64,6,128]{3,2,1,0:T(8,128)}, u32[]{:S(2)}, u32[]{:S(2)}) collective-permute-start(f32[1,64,6,128]{3,2,1,0:T(8,128)} %slice.82), channel_id=1, source_target_pairs={{4,0},{8,4},{12,8},{16,12},{20,16},{24,20},{28,24},{32,28},{36,32}... | collective-permute-start | bytes 589832 | tf_op jit(solution)/shard_map/ppermute | solution.py:20
  72.7 7.1 %collective-permute-start.5 = (f32[1,64,6,128]{3,2,1,0:T(8,128)}, f32[1,64,6,128]{3,2,1,0:T(8,128)}, u32[]{:S(2)}, u32[]{:S(2)}) collective-permute-start(f32[1,64,6,128]{3,2,1,0:T(8,128)} %slice.80), channel_id=1, source_target_pairs={{0,4},{4,8},{8,12},{12,16},{16,20},{20,24},{24,28},{28,32},{32,36}... | collective-permute-start | bytes 589832 | tf_op jit(solution)/shard_map/ppermute | solution.py:17
  79.8 2.1 %reshape_reshape.3 = bf16[512,3,128]{2,1,0:T(4,128)(2,1)} reshape(bf16[4,384,128]{2,1,0:T(8,128)(2,1)} %copy-done.1) | data formatting | bytes 786432 | tf_op jit(solution)/shard_map/reshape;reshape | solution.py:142
  81.9 1.6 %copy.39 = f32[512,768]{0,1:T(8,128)} copy(f32[512,768]{1,0:T(8,128)S(1)} %fusion.37) | data formatting | bytes 3145728 | tf_op jit(solution)/shard_map/dot_general | solution.py:103
  83.5 1.8 %copy.41 = bf16[512,3,128]{2,0,1:T(8,128)(2,1)} copy(bf16[512,3,128]{2,1,0:T(4,128)(2,1)} %reshape_reshape.3) | data formatting | bytes 786432
  85.4 1.9 %copy.40 = f32[512,6,128]{2,0,1:T(8,128)S(1)} copy(f32[512,6,128]{0,2,1:T(8,128)} %bitcast.74) | data formatting | bytes 3145728 | tf_op jit(solution)/shard_map/reshape | solution.py:105
  87.3 1.1 %pad_maximum_fusion = f32[2,64,6,128]{3,2,1,0:T(8,128)S(1)} fusion(f32[1,64,6,128]{3,2,1,0:T(8,128)} %collective-permute-done.6, f32[1,64,6,128]{3,2,1,0:T(8,128)} %collective-permute-done.5), kind=kLoop, calls=%fused_computation.15 | loop fusion | flops 98304 | bytes 786432 | tf_op jit(solution)/shard_map/stack | solution.py:114
  88.6 1.2 %copy.37 = f32[768,224]{1,0:T(8,128)} copy(f32[768,224]{0,1:T(8,128)S(1)} %maximum_bitcast_fusion) | data formatting | bytes 1376256 | tf_op jit(solution)/shard_map/dot_general | solution.py:136
  89.8 3.2 %divide_convert_fusion = bf16[512,6,128]{2,0,1:T(8,128)(2,1)} fusion(f32[512,6,128]{2,0,1:T(8,128)S(1)} %copy.40, f32[6,128,224]{2,1,0:T(8,128)} %bitcast.78, f32[512]{0:T(512)S(1)} %copy-done.7, pred[512]{0:T(512)(128)(4,1)S(1)} %broadcast_compare_fusion, s32[224]{0:T(256)S(1)} %bitcast.86), kind=kOutput, calls=%fused_computation.5 | convolution fusion | flops 1058373632 | bytes 3050880 | tf_op jit(solution)/shard_map/dot_general | solution.py:136
  (75 shorter events, 10.9 us)
Async XLA Ops:
  0.6 20.8 %copy-start = (bf16[4,384,384]{2,1,0:T(8,128)(2,1)S(1)}, bf16[4,384,384]{2,1,0:T(8,128)(2,1)}, u32[]{:S(2)}) copy-start(bf16[4,384,384]{2,1,0:T(8,128)(2,1)} %param.15) | copy-start | bytes 3538948
  0.6 3.8 %collective-permute-start = (f32[24,128]{1,0:T(8,128)}, f32[24,128]{1,0:T(8,128)S(1)}, u32[]{:S(2)}, u32[]{:S(2)}) collective-permute-start(f32[24,128]{1,0:T(8,128)} %param.11), channel_id=1, source_target_pairs={{0,1},{1,2},{2,3},{3,0},{4,5},{5,6},{6,7},{7,4},{8,9},{9,10},{10,1... | collective-permute-start | bytes 36872 | tf_op jit(solution)/shard_map/ppermute | solution.py:60
  1.9 6.1 %collective-permute-start.2 = (f32[24,128]{1,0:T(8,128)}, f32[24,128]{1,0:T(8,128)S(1)}, u32[]{:S(2)}, u32[]{:S(2)}) collective-permute-start(f32[24,128]{1,0:T(8,128)} %param.11), channel_id=1, source_target_pairs={{0,3},{1,0},{2,1},{3,2},{4,7},{5,4},{6,5},{7,6},{8,11},{9,8},{10,9... | collective-permute-start | bytes 36872 | tf_op jit(solution)/shard_map/ppermute | solution.py:63
  4.5 2.8 %collective-permute-start.1 = (f32[24,128]{1,0:T(8,128)S(1)}, f32[24,128]{1,0:T(8,128)S(1)}, u32[]{:S(2)}, u32[]{:S(2)}) collective-permute-start(f32[24,128]{1,0:T(8,128)S(1)} %collective-permute-done), channel_id=1, source_target_pairs={{0,1},{1,2},{2,3},{3,0},{4,5},{5,6},{6,7},{7,4},{8,9},{9,10},{10,1... | collective-permute-start | bytes 36872 | tf_op jit(solution)/shard_map/ppermute | solution.py:60
  8.8 11.9 %collective-permute-start.4 = (f32[96,128]{1,0:T(8,128)S(1)}, f32[96,128]{1,0:T(8,128)S(1)}, u32[]{:S(2)}, u32[]{:S(2)}) collective-permute-start(f32[96,128]{1,0:T(8,128)S(1)} %constant_dynamic-slice_fusion), channel_id=1, source_target_pairs={{4,0},{8,4},{12,8},{16,12},{20,16},{24,20},{28,24},{32,28},{36,32}... | collective-permute-start | bytes 147464 | tf_op jit(solution)/shard_map/ppermute | solution.py:20
  12.8 7.9 %collective-permute-start.3 = (f32[96,128]{1,0:T(8,128)S(1)}, f32[96,128]{1,0:T(8,128)S(1)}, u32[]{:S(2)}, u32[]{:S(2)}) collective-permute-start(f32[96,128]{1,0:T(8,128)S(1)} %constant_dynamic-slice_fusion), channel_id=1, source_target_pairs={{0,4},{4,8},{8,12},{12,16},{16,20},{20,24},{24,28},{28,32},{32,36}... | collective-permute-start | bytes 147464 | tf_op jit(solution)/shard_map/ppermute | solution.py:17
  20.0 0.9 copy-start.4
  22.2 4.1 %copy-start.1 = (bf16[4,384,128]{2,1,0:T(8,128)(2,1)}, bf16[4,384,128]{2,1,0:T(8,128)(2,1)S(1)}, u32[]{:S(2)}) copy-start(bf16[4,384,128]{2,1,0:T(8,128)(2,1)S(1)} %copy.32) | copy-start | bytes 1179652
  26.3 0.7 copy-start.6
  27.7 3.4 %copy-start.5 = (s32[1,224]{1,0:T(1,128)S(1)}, s32[1,224]{1,0:T(1,128)}, u32[]{:S(2)}) copy-start(s32[1,224]{1,0:T(1,128)} %param.20) | copy-start | bytes 2692
  32.1 7.7 %collective-permute-start.9 = (f32[1,2,8,6,128]{4,2,3,1,0:T(8,128)S(1)}, f32[1,2,8,6,128]{4,2,3,1,0:T(8,128)S(1)}, u32[]{:S(2)}, u32[]{:S(2)}) collective-permute-start(f32[1,2,8,6,128]{4,2,3,1,0:T(8,128)S(1)} %get-tuple-element.12), channel_id=1, source_target_pairs={{0,4},{4,8},{8,12},{12,16},{16,20},{20,24},{24,28},{28,32},{32,36}... | collective-permute-start | bytes 147464 | tf_op jit(solution)/shard_map/ppermute | solution.py:17
  37.9 8.7 %collective-permute-start.10 = (f32[1,2,8,6,128]{4,2,3,1,0:T(8,128)S(1)}, f32[1,2,8,6,128]{4,2,3,1,0:T(8,128)S(1)}, u32[]{:S(2)}, u32[]{:S(2)}) collective-permute-start(f32[1,2,8,6,128]{4,2,3,1,0:T(8,128)S(1)} %get-tuple-element.13), channel_id=1, source_target_pairs={{4,0},{8,4},{12,8},{16,12},{20,16},{24,20},{28,24},{32,28},{36,32}... | collective-permute-start | bytes 147464 | tf_op jit(solution)/shard_map/ppermute | solution.py:20
  46.7 5.7 %collective-permute-start.11 = (f32[4,1,8,6,128]{4,2,3,1,0:T(8,128)S(1)}, f32[4,1,8,6,128]{4,2,3,1,0:T(8,128)S(1)}, u32[]{:S(2)}, u32[]{:S(2)}) collective-permute-start(f32[4,1,8,6,128]{4,2,3,1,0:T(8,128)S(1)} %get-tuple-element.14), channel_id=1, source_target_pairs={{0,1},{1,2},{2,3},{4,5},{5,6},{6,7},{8,9},{9,10},{10,11},{12,13},{... | collective-permute-start | bytes 294920 | tf_op jit(solution)/shard_map/ppermute | solution.py:17
  49.5 5.4 %collective-permute-start.12 = (f32[4,1,8,6,128]{4,2,3,1,0:T(8,128)S(1)}, f32[4,1,8,6,128]{4,2,3,1,0:T(8,128)S(1)}, u32[]{:S(2)}, u32[]{:S(2)}) collective-permute-start(f32[4,1,8,6,128]{4,2,3,1,0:T(8,128)S(1)} %get-tuple-element.15), channel_id=1, source_target_pairs={{1,0},{2,1},{3,2},{5,4},{6,5},{7,6},{9,8},{10,9},{11,10},{13,12},{... | collective-permute-start | bytes 294920 | tf_op jit(solution)/shard_map/ppermute | solution.py:20
  57.9 5.9 %collective-permute-start.8 = (f32[1,32,6,128]{3,2,1,0:T(8,128)}, f32[1,32,6,128]{3,2,1,0:T(8,128)S(1)}, u32[]{:S(2)}, u32[]{:S(2)}) collective-permute-start(f32[1,32,6,128]{3,2,1,0:T(8,128)} %slice.87), channel_id=1, source_target_pairs={{1,0},{2,1},{3,2},{5,4},{6,5},{7,6},{9,8},{10,9},{11,10},{13,12},{... | collective-permute-start | bytes 294920 | tf_op jit(solution)/shard_map/ppermute | solution.py:20
  60.6 5.9 %collective-permute-start.7 = (f32[1,32,6,128]{3,2,1,0:T(8,128)}, f32[1,32,6,128]{3,2,1,0:T(8,128)S(1)}, u32[]{:S(2)}, u32[]{:S(2)}) collective-permute-start(f32[1,32,6,128]{3,2,1,0:T(8,128)} %slice.85), channel_id=1, source_target_pairs={{0,1},{1,2},{2,3},{4,5},{5,6},{6,7},{8,9},{9,10},{10,11},{12,13},{... | collective-permute-start | bytes 294920 | tf_op jit(solution)/shard_map/ppermute | solution.py:17
  70.7 16.5 %collective-permute-start.6 = (f32[1,64,6,128]{3,2,1,0:T(8,128)}, f32[1,64,6,128]{3,2,1,0:T(8,128)}, u32[]{:S(2)}, u32[]{:S(2)}) collective-permute-start(f32[1,64,6,128]{3,2,1,0:T(8,128)} %slice.82), channel_id=1, source_target_pairs={{4,0},{8,4},{12,8},{16,12},{20,16},{24,20},{28,24},{32,28},{36,32}... | collective-permute-start | bytes 589832 | tf_op jit(solution)/shard_map/ppermute | solution.py:20
  72.7 14.6 %collective-permute-start.5 = (f32[1,64,6,128]{3,2,1,0:T(8,128)}, f32[1,64,6,128]{3,2,1,0:T(8,128)}, u32[]{:S(2)}, u32[]{:S(2)}) collective-permute-start(f32[1,64,6,128]{3,2,1,0:T(8,128)} %slice.80), channel_id=1, source_target_pairs={{0,4},{4,8},{8,12},{12,16},{16,20},{20,24},{24,28},{28,32},{32,36}... | collective-permute-start | bytes 589832 | tf_op jit(solution)/shard_map/ppermute | solution.py:17
  87.3 1.3 %copy-start.2 = (f32[64,768]{1,0:T(8,128)S(1)}, f32[64,768]{1,0:T(8,128)}, u32[]{:S(2)}) copy-start(f32[64,768]{1,0:T(8,128)} %get-tuple-element.7) | copy-start | bytes 589828
  87.3 1.3 %copy-start.3 = (f32[32,768]{1,0:T(8,128)S(1)}, f32[32,768]{1,0:T(8,128)}, u32[]{:S(2)}) copy-start(f32[32,768]{1,0:T(8,128)} %get-tuple-element.10) | copy-start | bytes 294916
  88.5 1.3 %copy-start.7 = (f32[512]{0:T(512)S(1)}, f32[512]{0:T(512)}, u32[]{:S(2)}) copy-start(f32[512]{0:T(512)} %param.21) | copy-start | bytes 6148
